TPU v7x, 512 devices: a whole 4x8x8 slice. The times are simulated.
512 devices in a mesh: rows: 64 (over y, x, core), rhs: 8 (over z).
Axes of the slice: x: 4, y: 8, z: 8, core: 2. Of those that a mesh axis runs over, the one named last changes fastest.
Arguments:
- right_side: float32 [64, 32768], P('rhs', 'rows'), may hold values from -6 to 6
- tiles: float32 [512, 7, 64, 64], P('rows'), may hold values from -2 to 5.5, as said below
- pivots: float32 [512, 64, 64], P('rows'), may hold values from -0.05 to 0.8, as said below
- columns: int32 [512, 7], P('rows'), may hold values from 0 to 511, as said below
Outputs:
- solution: float32 [64, 32768], P('rhs', 'rows')
- residual: float32 [64, 32768], P('rhs', 'rows')
Inputs may be any that keep to these rules, and one draw needn't show every extreme that they name: columns[i, 0] = i. The other six columns of block row i are i - o and i + o for three offsets o shared by all block rows, the largest of them exactly 8, in an order of the slots drawn for each block row; a column that would fall outside 0 to 511 is i itself. tiles[i, 0] is the diagonal tile of block row i; A is symmetric positive definite: the tile of block row i in a slot whose column j differs from i is the transpose of the tile of block row j in its slot whose column is i. Every pivots[i] is symmetric positive definite.
All inputs are finite; a program needn't handle non-finite values.
Results may differ from a plain program's by a relative error of at most 0.0003.
Values sent between devices are 32-bit elements; how exact they have to be, the bound alone decides.
A program may use at most 64 MiB of HBM per device.

v0:
```python
import jax
import jax.numpy as jnp
from jax import lax
from jax.sharding import PartitionSpec as P

SPAN = 8
ITERS = 2


def passed_along(value, axis, steps):
    count = lax.axis_size(axis)
    first, last = (max(0, -steps), min(count, count - steps))
    return lax.ppermute(value, axis, [(source, source + steps) for source in range(first, last)])


def extended_2(block, sides, width):
    for axis, dim in sides:
        count = lax.axis_size(axis)
        forward = [(i, i + 1) for i in range(count - 1)]
        backward = [(target, source) for source, target in forward]
        low = lax.ppermute(
            lax.slice_in_dim(block, block.shape[dim] - width, None, axis=dim), axis, forward
        )
        high = lax.ppermute(lax.slice_in_dim(block, 0, width, axis=dim), axis, backward)
        block = jnp.concatenate([low, block, high], axis=dim)
    return block


def inner(left, right):
    return jnp.dot(left, right.T, precision=lax.Precision.HIGHEST)


def chol_solve(factor, values):
    middle = lax.linalg.triangular_solve(factor, values, left_side=True, lower=True)
    return lax.linalg.triangular_solve(factor, middle, left_side=True, lower=True, transpose_a=True)


def shards(right_side, tiles, pivots, columns):
    count = right_side.shape[0]
    shard_rows = tiles.shape[0]
    width = tiles.shape[2]
    cells = shard_rows * width
    where_row = lax.axis_index("rows")
    start = where_row * shard_rows
    position = where_row % SPAN
    block_low = (where_row - position) * shard_rows
    block_high = block_low + SPAN * shard_rows
    global_rows = start + jnp.arange(shard_rows, dtype=jnp.int32)
    lower = (columns < global_rows[:, None]) & (columns >= block_low)
    upper = (columns > global_rows[:, None]) & (columns < block_high)
    lower_tiles = tiles * lower[:, :, None, None].astype(tiles.dtype)
    upper_tiles = tiles * upper[:, :, None, None].astype(tiles.dtype)
    forward_cols = jnp.clip(columns - start + shard_rows, 0, 2 * shard_rows - 1)
    backward_cols = jnp.clip(columns - start, 0, 2 * shard_rows - 1)
    halo_cols = columns - start + shard_rows
    from_below = (position != 0).astype(jnp.float32)
    from_above = (position != SPAN - 1).astype(jnp.float32)

    def forward_local(source, incoming):
        extended = jnp.concatenate([incoming, jnp.zeros_like(source)], axis=1)

        def forward_one_row(row, extended):
            picked = jnp.take(extended, forward_cols[row], axis=1)
            summed = jnp.einsum(
                "kab,ckb->ca", lower_tiles[row], picked, precision=lax.Precision.HIGHEST
            )
            remain = source[:, row] - summed
            value = jnp.einsum("ab,cb->ca", pivots[row], remain, precision=lax.Precision.HIGHEST)
            return lax.dynamic_update_slice_in_dim(extended, value[:, None], shard_rows + row, 1)

        extended = lax.fori_loop(0, shard_rows, forward_one_row, extended)
        return extended[:, shard_rows:]

    def backward_local(source, incoming):
        extended = jnp.concatenate([jnp.zeros_like(source), incoming], axis=1)

        def backward_one_row(turn, extended):
            row = shard_rows - 1 - turn
            picked = jnp.take(extended, backward_cols[row], axis=1)
            summed = jnp.einsum(
                "kab,ckb->ca", upper_tiles[row], picked, precision=lax.Precision.HIGHEST
            )
            value = source[:, row] - jnp.einsum(
                "ab,cb->ca", pivots[row], summed, precision=lax.Precision.HIGHEST
            )
            return lax.dynamic_update_slice_in_dim(extended, value[:, None], row, 1)

        extended = lax.fori_loop(0, shard_rows, backward_one_row, extended)
        return extended[:, :shard_rows]

    def precondition(vector):
        source = vector.reshape(count, shard_rows, width)
        lowered = forward_local(source, jnp.zeros_like(source))
        for turn in range(SPAN - 1):
            incoming = passed_along(lowered, "rows", 1) * from_below
            lowered = forward_local(source, incoming)
        result = backward_local(lowered, jnp.zeros_like(lowered))
        for turn in range(SPAN - 1):
            incoming = passed_along(result, "rows", -1) * from_above
            result = backward_local(lowered, incoming)
        return result.reshape(count, cells)

    solution = jnp.zeros_like(right_side)
    residual = right_side
    direction = precondition(residual)
    for turn in range(ITERS):
        blocks = extended_2(direction, (("rows", 1),), cells).reshape(count, 3 * shard_rows, width)
        apply_picked = jnp.take(blocks, halo_cols, axis=1)
        image = jnp.einsum(
            "ikab,cikb->cia", tiles, apply_picked, precision=lax.Precision.HIGHEST
        ).reshape(count, cells)
        every_direction = lax.all_gather(direction, "rhs", axis=0, tiled=True)
        partial_pq = inner(every_direction, image)
        partial_pr = inner(every_direction, residual)
        summed_pq, summed_pr = lax.psum((partial_pq, partial_pr), "rows")
        gram = lax.all_gather(summed_pq, "rhs", axis=1, tiled=True)
        factor = jnp.linalg.cholesky(0.5 * (gram + gram.T))
        alpha = chol_solve(factor, summed_pr)
        change = jnp.dot(alpha.T, every_direction, precision=lax.Precision.HIGHEST)
        solution = solution + change
        if turn + 1 < ITERS:
            every_image = lax.all_gather(image, "rhs", axis=0, tiled=True)
            residual = residual - jnp.dot(alpha.T, every_image, precision=lax.Precision.HIGHEST)
            preconditioned = precondition(residual)
            summed_qz = lax.psum(inner(every_image, preconditioned), "rows")
            beta = -chol_solve(factor, summed_qz)
            direction = preconditioned + jnp.dot(
                beta.T, every_direction, precision=lax.Precision.HIGHEST
            )
        else:
            every_image = lax.all_gather(image, "rhs", axis=0, tiled=True)
            residual = residual - jnp.dot(alpha.T, every_image, precision=lax.Precision.HIGHEST)
    return (solution, residual)


def solution(mesh):
    return jax.shard_map(
        shards,
        mesh=mesh,
        in_specs=(
            P("rhs", "rows"),
            P("rows", None, None, None),
            P("rows", None, None),
            P("rows", None),
        ),
        out_specs=(P("rhs", "rows"), P("rhs", "rows")),
        check_vma=False,
    )
```

profile of v0, /device:TPU:32, one launch (start us, length us, event | category | flops | bytes accessed | tf_op | source)
XLA Modules:
  0.0 1239.9 jit_solution(11222102633937518841)
XLA Ops:
  6.0 16.7 %while.480 = (s32[]{:T(128)}, f32[8,16,64]{2,0,1:T(8,128)S(1)}, f32[8,8,64]{2,0,1:T(8,128)S(1)}, s32[8,7]{1,0:T(8,128)S(1)}, f32[8,7,64,64]{3,2,1,0:T(8,128)}, /...) while((s32[]{:T(128)}, f32[8,16,64]{2,0,1:T(8,128)S(1)}, ...), condition=%wide.region_1.3_spmd, body=%wide.region_0.2_spmd.sunk | while | flops 3150896 | bytes 322845 | solution.py:71
  31.3 16.7 %while.481 = (s32[]{:T(128)}, f32[8,16,64]{2,0,1:T(8,128)S(1)}, f32[8,8,64]{2,0,1:T(8,128)S(1)}, s32[8,7]{1,0:T(8,128)S(1)}, f32[8,7,64,64]{3,2,1,0:T(8,128)}, /...) while((s32[]{:T(128)}, f32[8,16,64]{2,0,1:T(8,128)S(1)}, ...), condition=%wide.region_3.5_spmd, body=%wide.region_2.4_spmd.sunk | while | flops 3150896 | bytes 322845 | solution.py:71
  56.6 16.7 %while.482 = (s32[]{:T(128)}, f32[8,16,64]{2,0,1:T(8,128)S(1)}, f32[8,8,64]{2,0,1:T(8,128)S(1)}, s32[8,7]{1,0:T(8,128)S(1)}, f32[8,7,64,64]{3,2,1,0:T(8,128)}, /...) while((s32[]{:T(128)}, f32[8,16,64]{2,0,1:T(8,128)S(1)}, ...), condition=%wide.region_5.7_spmd, body=%wide.region_4.6_spmd.sunk | while | flops 3150896 | bytes 322845 | solution.py:71
  81.9 16.7 %while.483 = (s32[]{:T(128)}, f32[8,16,64]{2,0,1:T(8,128)S(1)}, f32[8,8,64]{2,0,1:T(8,128)S(1)}, s32[8,7]{1,0:T(8,128)S(1)}, f32[8,7,64,64]{3,2,1,0:T(8,128)}, /...) while((s32[]{:T(128)}, f32[8,16,64]{2,0,1:T(8,128)S(1)}, ...), condition=%wide.region_7.9_spmd, body=%wide.region_6.8_spmd.sunk | while | flops 3150896 | bytes 322845 | solution.py:71
  107.2 16.7 %while.484 = (s32[]{:T(128)}, f32[8,16,64]{2,0,1:T(8,128)S(1)}, f32[8,8,64]{2,0,1:T(8,128)S(1)}, s32[8,7]{1,0:T(8,128)S(1)}, f32[8,7,64,64]{3,2,1,0:T(8,128)}, /...) while((s32[]{:T(128)}, f32[8,16,64]{2,0,1:T(8,128)S(1)}, ...), condition=%wide.region_9.11_spmd, body=%wide.region_8.10_spmd.sunk | while | flops 3150896 | bytes 322845 | solution.py:71
  132.5 16.7 %while.485 = (s32[]{:T(128)}, f32[8,16,64]{2,0,1:T(8,128)S(1)}, f32[8,8,64]{2,0,1:T(8,128)S(1)}, s32[8,7]{1,0:T(8,128)S(1)}, f32[8,7,64,64]{3,2,1,0:T(8,128)}, /...) while((s32[]{:T(128)}, f32[8,16,64]{2,0,1:T(8,128)S(1)}, ...), condition=%wide.region_11.13_spmd, body=%wide.region_10.12_spmd.sunk | while | flops 3150896 | bytes 322845 | solution.py:71
  157.8 16.7 %while.486 = (s32[]{:T(128)}, f32[8,16,64]{2,0,1:T(8,128)S(1)}, f32[8,8,64]{2,0,1:T(8,128)S(1)}, s32[8,7]{1,0:T(8,128)S(1)}, f32[8,7,64,64]{3,2,1,0:T(8,128)}, /...) while((s32[]{:T(128)}, f32[8,16,64]{2,0,1:T(8,128)S(1)}, ...), condition=%wide.region_13.15_spmd, body=%wide.region_12.14_spmd.sunk | while | flops 3150896 | bytes 322845 | solution.py:71
  183.1 16.7 %while.487 = (s32[]{:T(128)}, f32[8,16,64]{2,0,1:T(8,128)S(1)}, f32[8,8,64]{2,0,1:T(8,128)S(1)}, s32[8,7]{1,0:T(8,128)S(1)}, f32[8,7,64,64]{3,2,1,0:T(8,128)}, /...) while((s32[]{:T(128)}, f32[8,16,64]{2,0,1:T(8,128)S(1)}, ...), condition=%wide.region_15.17_spmd, body=%wide.region_14.16_spmd.sunk | while | flops 3150896 | bytes 322845 | solution.py:71
  337.6 30.9 %all_gather.18 = f32[64,512]{1,0:T(8,128)S(1)} all-gather(f32[8,512]{1,0:T(8,128)S(1)} %reshape.66), channel_id=1, replica_groups=mesh['rows'=64,'rhs'=8] {'rhs'}, dimensions={0}, use_global_device_ids=true | all-gather | bytes 147456 | tf_op jit(solution)/shard_map/all_gather | solution.py:112
  373.2 24.6 %all_gather.20 = f32[64,512]{1,0:T(8,128)S(1)} all-gather(f32[8,512]{1,0:T(8,128)S(1)} %reshape.67), channel_id=1, replica_groups=mesh['rows'=64,'rhs'=8] {'rhs'}, dimensions={0}, use_global_device_ids=true | all-gather | bytes 147456 | tf_op jit(solution)/shard_map/all_gather | solution.py:122
  397.8 126.1 %all-reduce.29 = (f32[64,8]{0,1:T(8,128)S(1)}, f32[64,8]{0,1:T(8,128)S(1)}) all-reduce(f32[64,8]{0,1:T(8,128)S(1)} %fusion.476, f32[64,8]{0,1:T(8,128)S(1)} %fusion.475), channel_id=1, replica_groups=mesh['rows'=64,'rhs'=8] {'rows'}, use_global_device_ids=true, to_apply=%region_35.39 | all-reduce | flops 1024 | bytes 8192 | tf_op jit(solution)/shard_map/psum | solution.py:115
  523.9 24.5 %all_gather.19 = f32[64,64]{0,1:T(8,128)S(1)} all-gather(f32[64,8]{0,1:T(8,128)S(1)} %get-tuple-element.5610), channel_id=1, replica_groups=mesh['rows'=64,'rhs'=8] {'rhs'}, dimensions={1}, use_global_device_ids=true | all-gather | bytes 18432 | tf_op jit(solution)/shard_map/all_gather | solution.py:116
  561.3 16.7 %while.496 = (s32[]{:T(128)}, f32[8,16,64]{2,0,1:T(8,128)S(1)}, f32[8,8,64]{2,0,1:T(8,128)S(1)}, s32[8,7]{1,0:T(8,128)S(1)}, f32[8,7,64,64]{3,2,1,0:T(8,128)}, /...) while((s32[]{:T(128)}, f32[8,16,64]{2,0,1:T(8,128)S(1)}, ...), condition=%wide.region_37.43_spmd, body=%wide.region_36.42_spmd.sunk | while | flops 3150896 | bytes 322845 | solution.py:71
  586.6 16.7 %while.497 = (s32[]{:T(128)}, f32[8,16,64]{2,0,1:T(8,128)S(1)}, f32[8,8,64]{2,0,1:T(8,128)S(1)}, s32[8,7]{1,0:T(8,128)S(1)}, f32[8,7,64,64]{3,2,1,0:T(8,128)}, /...) while((s32[]{:T(128)}, f32[8,16,64]{2,0,1:T(8,128)S(1)}, ...), condition=%wide.region_39.45_spmd, body=%wide.region_38.44_spmd.sunk | while | flops 3150896 | bytes 322845 | solution.py:71
  611.9 16.7 %while.498 = (s32[]{:T(128)}, f32[8,16,64]{2,0,1:T(8,128)S(1)}, f32[8,8,64]{2,0,1:T(8,128)S(1)}, s32[8,7]{1,0:T(8,128)S(1)}, f32[8,7,64,64]{3,2,1,0:T(8,128)}, /...) while((s32[]{:T(128)}, f32[8,16,64]{2,0,1:T(8,128)S(1)}, ...), condition=%wide.region_41.47_spmd, body=%wide.region_40.46_spmd.sunk | while | flops 3150896 | bytes 322845 | solution.py:71
  662.5 16.7 %while.500 = (s32[]{:T(128)}, f32[8,16,64]{2,0,1:T(8,128)S(1)}, f32[8,8,64]{2,0,1:T(8,128)S(1)}, s32[8,7]{1,0:T(8,128)S(1)}, f32[8,7,64,64]{3,2,1,0:T(8,128)}, /...) while((s32[]{:T(128)}, f32[8,16,64]{2,0,1:T(8,128)S(1)}, ...), condition=%wide.region_45.51_spmd, body=%wide.region_44.50_spmd.sunk | while | flops 3150896 | bytes 322845 | solution.py:71
  687.8 16.7 %while.501 = (s32[]{:T(128)}, f32[8,16,64]{2,0,1:T(8,128)S(1)}, f32[8,8,64]{2,0,1:T(8,128)S(1)}, s32[8,7]{1,0:T(8,128)S(1)}, f32[8,7,64,64]{3,2,1,0:T(8,128)}, /...) while((s32[]{:T(128)}, f32[8,16,64]{2,0,1:T(8,128)S(1)}, ...), condition=%wide.region_47.53_spmd, body=%wide.region_46.52_spmd.sunk | while | flops 3150896 | bytes 322845 | solution.py:71
  713.1 16.7 %while.502 = (s32[]{:T(128)}, f32[8,16,64]{2,0,1:T(8,128)S(1)}, f32[8,8,64]{2,0,1:T(8,128)S(1)}, s32[8,7]{1,0:T(8,128)S(1)}, f32[8,7,64,64]{3,2,1,0:T(8,128)}, /...) while((s32[]{:T(128)}, f32[8,16,64]{2,0,1:T(8,128)S(1)}, ...), condition=%wide.region_49.55_spmd, body=%wide.region_48.54_spmd.sunk | while | flops 3150896 | bytes 322845 | solution.py:71
  738.4 16.7 %while.503 = (s32[]{:T(128)}, f32[8,16,64]{2,0,1:T(8,128)S(1)}, f32[8,8,64]{2,0,1:T(8,128)S(1)}, s32[8,7]{1,0:T(8,128)S(1)}, f32[8,7,64,64]{3,2,1,0:T(8,128)}, /...) while((s32[]{:T(128)}, f32[8,16,64]{2,0,1:T(8,128)S(1)}, ...), condition=%wide.region_51.57_spmd, body=%wide.region_50.56_spmd.sunk | while | flops 3150896 | bytes 322845 | solution.py:71
  884.2 129.3 %psum.37 = f32[64,8]{0,1:T(8,128)S(1)} all-reduce(f32[64,8]{0,1:T(8,128)S(1)} %fusion.478), channel_id=1, replica_groups=mesh['rows'=64,'rhs'=8] {'rows'}, use_global_device_ids=true, to_apply=%region_68.74 | all-reduce | flops 512 | bytes 4096 | tf_op jit(solution)/shard_map/psum | solution.py:125
  1022.8 24.6 %all_gather.21 = f32[64,512]{1,0:T(8,128)S(1)} all-gather(f32[8,512]{1,0:T(8,128)S(1)} %convolution_add_fusion.1), channel_id=1, replica_groups=mesh['rows'=64,'rhs'=8] {'rhs'}, dimensions={0}, use_global_device_ids=true | all-gather | bytes 147456 | tf_op jit(solution)/shard_map/all_gather | solution.py:112
  1050.5 24.6 %all_gather.23 = f32[64,512]{1,0:T(8,128)S(1)} all-gather(f32[8,512]{1,0:T(8,128)S(1)} %reshape.71), channel_id=1, replica_groups=mesh['rows'=64,'rhs'=8] {'rhs'}, dimensions={0}, use_global_device_ids=true | all-gather | bytes 147456 | tf_op jit(solution)/shard_map/all_gather | solution.py:131
  1075.2 126.1 %all-reduce.28 = (f32[64,8]{0,1:T(8,128)S(1)}, f32[64,8]{0,1:T(8,128)S(1)}) all-reduce(f32[64,8]{0,1:T(8,128)S(1)} %fusion.480, f32[64,8]{0,1:T(8,128)S(1)} %fusion.479), channel_id=1, replica_groups=mesh['rows'=64,'rhs'=8] {'rows'}, use_global_device_ids=true, to_apply=%region_70.76 | all-reduce | flops 1024 | bytes 8192 | tf_op jit(solution)/shard_map/psum | solution.py:115
  1201.3 24.5 %all_gather.22 = f32[64,64]{0,1:T(8,128)S(1)} all-gather(f32[64,8]{0,1:T(8,128)S(1)} %get-tuple-element.5608), channel_id=1, replica_groups=mesh['rows'=64,'rhs'=8] {'rhs'}, dimensions={1}, use_global_device_ids=true | all-gather | bytes 18432 | tf_op jit(solution)/shard_map/all_gather | solution.py:116
  (1523 shorter events, 860.4 us)
Async XLA Ops:
  22.7 8.6 collective-permute-start
  48.0 8.6 collective-permute-start.1
  73.3 8.6 collective-permute-start.2
  98.6 8.6 collective-permute-start.3
  123.9 8.6 collective-permute-start.4
  149.2 8.6 collective-permute-start.5
  174.5 8.6 collective-permute-start.6
  221.8 8.6 collective-permute-start.8
  257.4 8.6 collective-permute-start.10
  293.0 8.6 collective-permute-start.12
  328.7 40.0 %collective-permute-start.14 = (f32[8,512]{1,0:T(8,128)S(1)}, f32[8,512]{1,0:T(8,128)S(1)}, u32[]{:S(2)}, u32[]{:S(2)}) collective-permute-start(f32[8,512]{1,0:T(8,128)S(1)} %reshape.66), channel_id=1, source_target_pairs={{0,8},{8,16},{16,24},{24,32},{32,40},{40,48},{48,56},{56,64},{64,7... | collective-permute-start | bytes 49160 | tf_op jit(solution)/shard_map/ppermute | solution.py:21
  330.6 38.2 %collective-permute-start.15 = (f32[8,512]{1,0:T(8,128)S(1)}, f32[8,512]{1,0:T(8,128)S(1)}, u32[]{:S(2)}, u32[]{:S(2)}) collective-permute-start(f32[8,512]{1,0:T(8,128)S(1)} %reshape.66), channel_id=1, source_target_pairs={{8,0},{16,8},{24,16},{32,24},{40,32},{48,40},{56,48},{64,56},{72,6... | collective-permute-start | bytes 49160 | tf_op jit(solution)/shard_map/ppermute | solution.py:24
  578.0 8.6 collective-permute-start.16
  603.3 8.6 collective-permute-start.17
  628.6 8.6 collective-permute-start.18
  653.9 8.6 collective-permute-start.19
  679.2 8.6 collective-permute-start.20
  704.5 8.6 collective-permute-start.21
  729.8 8.6 collective-permute-start.22
  777.1 8.6 collective-permute-start.24
  794.9 8.6 collective-permute-start.25
  812.7 8.6 collective-permute-start.26
  1013.9 33.6 %collective-permute-start.30 = (f32[8,512]{1,0:T(8,128)S(1)}, f32[8,512]{1,0:T(8,128)S(1)}, u32[]{:S(2)}, u32[]{:S(2)}) collective-permute-start(f32[8,512]{1,0:T(8,128)S(1)} %convolution_add_fusion.1), channel_id=1, source_target_pairs={{0,8},{8,16},{16,24},{24,32},{32,40},{40,48},{48,56},{56,64},{64,7... | collective-permute-start | bytes 49160 | tf_op jit(solution)/shard_map/ppermute | solution.py:21
  1015.9 31.8 %collective-permute-start.31 = (f32[8,512]{1,0:T(8,128)S(1)}, f32[8,512]{1,0:T(8,128)S(1)}, u32[]{:S(2)}, u32[]{:S(2)}) collective-permute-start(f32[8,512]{1,0:T(8,128)S(1)} %convolution_add_fusion.1), channel_id=1, source_target_pairs={{8,0},{16,8},{24,16},{32,24},{40,32},{48,40},{56,48},{64,56},{72,6... | collective-permute-start | bytes 49160 | tf_op jit(solution)/shard_map/ppermute | solution.py:24
  (11 other events, 283.7 us)
where the time goes:
time: 1240 us
  blocking collectives  535 us (43%)
  matrix products  265 us (21%)
  local copies, waits for them, and re-layouts  146 us (12%)
  starting transfers between devices  133 us (11%)
  waiting for transfers between devices  114 us (9%)
  other arithmetic  39.3 us (3%)
    psum x2, blocking collectives, shards(): summed_pq, summed_pr = lax.psum((partial_pq, partial_pr), 'rows')  252 us
    dot_general x128, matrix products, forward_one_row(): jnp.einsum('kab,ckb->ca', lower_tiles[row], picked, precision=lax.Precisi...  162 us
    psum x1, blocking collectives, shards(): summed_qz = lax.psum(inner(every_image, preconditioned), 'rows')  129 us
    ppermute x28, starting transfers between devices, passed_along(): lax.ppermute(value, axis, [(source, source + steps) for source in range(f...  115 us
    ppermute x28, waiting for transfers between devices, passed_along(): lax.ppermute(value, axis, [(source, source + steps) for source in range(f...  114 us
    gather x128, local copies, waits for them, and re-layouts, forward_one_row(): picked = jnp.take(extended, forward_cols[row], axis=1)  70.9 us
    gather x128, local copies, waits for them, and re-layouts, backward_one_row(): picked = jnp.take(extended, backward_cols[row], axis=1)  70.9 us
    all_gather x2, blocking collectives, shards(): every_direction = lax.all_gather(direction, 'rhs', axis=0, tiled=True)  55.5 us
  transfers between devices with their start and end apart: 32, of which 28 were waited for; matrix products, arithmetic and copies ran while one was open for 0% of the time, Pallas kernels for 0%

commit v1 on v0

--- a/solution.py
+++ b/solution.py
@@ -122,7 +122,9 @@
             every_image = lax.all_gather(image, "rhs", axis=0, tiled=True)
             residual = residual - jnp.dot(alpha.T, every_image, precision=lax.Precision.HIGHEST)
             preconditioned = precondition(residual)
-            summed_qz = lax.psum(inner(every_image, preconditioned), "rows")
+            block_2 = inner(every_image, preconditioned)
+            parts = lax.all_gather(block_2, "rows")
+            summed_qz = jnp.sum(parts, axis=0)
             beta = -chol_solve(factor, summed_qz)
             direction = preconditioned + jnp.dot(
                 beta.T, every_direction, precision=lax.Precision.HIGHEST

time: 1240 us -> 1150 us (0.927)
  blocking collectives: 535 us -> 443 us
    psum x1 -> x0, blocking collectives: 129 us -> none  [shards(): summed_qz = lax.psum(inner(every_image, preconditioned), 'rows')]
    all_gather x0 -> x1, blocking collectives: none -> 37.4 us  [shards(): parts = lax.all_gather(block_2, 'rows')]
where the time goes in v1:
time: 1150 us
  blocking collectives  443 us (39%)
  matrix products  265 us (23%)
  local copies, waits for them, and re-layouts  146 us (13%)
  starting transfers between devices  133 us (12%)
  waiting for transfers between devices  114 us (10%)
  other arithmetic  39.3 us (3%)
    psum x2, blocking collectives, shards(): summed_pq, summed_pr = lax.psum((partial_pq, partial_pr), 'rows')  252 us
    dot_general x128, matrix products, forward_one_row(): jnp.einsum('kab,ckb->ca', lower_tiles[row], picked, precision=lax.Precisi...  162 us
    ppermute x28, starting transfers between devices, passed_along(): lax.ppermute(value, axis, [(source, source + steps) for source in range(f...  115 us
    ppermute x28, waiting for transfers between devices, passed_along(): lax.ppermute(value, axis, [(source, source + steps) for source in range(f...  114 us
    gather x128, local copies, waits for them, and re-layouts, forward_one_row(): picked = jnp.take(extended, forward_cols[row], axis=1)  70.9 us
    gather x128, local copies, waits for them, and re-layouts, backward_one_row(): picked = jnp.take(extended, backward_cols[row], axis=1)  70.9 us
    all_gather x2, blocking collectives, shards(): every_direction = lax.all_gather(direction, 'rhs', axis=0, tiled=True)  55.5 us
    all_gather x2, blocking collectives, shards(): every_image = lax.all_gather(image, 'rhs', axis=0, tiled=True)  49.2 us
  transfers between devices with their start and end apart: 32, of which 28 were waited for; matrix products, arithmetic and copies ran while one was open for 0% of the time, Pallas kernels for 0%

profile of v1, /device:TPU:32, one launch (start us, length us, event | category | flops | bytes accessed | tf_op | source)
XLA Modules:
  0.0 1148.1 jit_solution(8598031179956018081)
XLA Ops:
  6.0 16.7 %while.480 = (s32[]{:T(128)}, f32[8,16,64]{2,0,1:T(8,128)S(1)}, f32[8,8,64]{2,0,1:T(8,128)S(1)}, s32[8,7]{1,0:T(8,128)S(1)}, f32[8,7,64,64]{3,2,1,0:T(8,128)}, /...) while((s32[]{:T(128)}, f32[8,16,64]{2,0,1:T(8,128)S(1)}, ...), condition=%wide.region_1.3_spmd, body=%wide.region_0.2_spmd.sunk | while | flops 3150896 | bytes 322845 | solution.py:71
  31.3 16.7 %while.481 = (s32[]{:T(128)}, f32[8,16,64]{2,0,1:T(8,128)S(1)}, f32[8,8,64]{2,0,1:T(8,128)S(1)}, s32[8,7]{1,0:T(8,128)S(1)}, f32[8,7,64,64]{3,2,1,0:T(8,128)}, /...) while((s32[]{:T(128)}, f32[8,16,64]{2,0,1:T(8,128)S(1)}, ...), condition=%wide.region_3.5_spmd, body=%wide.region_2.4_spmd.sunk | while | flops 3150896 | bytes 322845 | solution.py:71
  56.6 16.7 %while.482 = (s32[]{:T(128)}, f32[8,16,64]{2,0,1:T(8,128)S(1)}, f32[8,8,64]{2,0,1:T(8,128)S(1)}, s32[8,7]{1,0:T(8,128)S(1)}, f32[8,7,64,64]{3,2,1,0:T(8,128)}, /...) while((s32[]{:T(128)}, f32[8,16,64]{2,0,1:T(8,128)S(1)}, ...), condition=%wide.region_5.7_spmd, body=%wide.region_4.6_spmd.sunk | while | flops 3150896 | bytes 322845 | solution.py:71
  81.9 16.7 %while.483 = (s32[]{:T(128)}, f32[8,16,64]{2,0,1:T(8,128)S(1)}, f32[8,8,64]{2,0,1:T(8,128)S(1)}, s32[8,7]{1,0:T(8,128)S(1)}, f32[8,7,64,64]{3,2,1,0:T(8,128)}, /...) while((s32[]{:T(128)}, f32[8,16,64]{2,0,1:T(8,128)S(1)}, ...), condition=%wide.region_7.9_spmd, body=%wide.region_6.8_spmd.sunk | while | flops 3150896 | bytes 322845 | solution.py:71
  107.2 16.7 %while.484 = (s32[]{:T(128)}, f32[8,16,64]{2,0,1:T(8,128)S(1)}, f32[8,8,64]{2,0,1:T(8,128)S(1)}, s32[8,7]{1,0:T(8,128)S(1)}, f32[8,7,64,64]{3,2,1,0:T(8,128)}, /...) while((s32[]{:T(128)}, f32[8,16,64]{2,0,1:T(8,128)S(1)}, ...), condition=%wide.region_9.11_spmd, body=%wide.region_8.10_spmd.sunk | while | flops 3150896 | bytes 322845 | solution.py:71
  132.5 16.7 %while.485 = (s32[]{:T(128)}, f32[8,16,64]{2,0,1:T(8,128)S(1)}, f32[8,8,64]{2,0,1:T(8,128)S(1)}, s32[8,7]{1,0:T(8,128)S(1)}, f32[8,7,64,64]{3,2,1,0:T(8,128)}, /...) while((s32[]{:T(128)}, f32[8,16,64]{2,0,1:T(8,128)S(1)}, ...), condition=%wide.region_11.13_spmd, body=%wide.region_10.12_spmd.sunk | while | flops 3150896 | bytes 322845 | solution.py:71
  157.8 16.7 %while.486 = (s32[]{:T(128)}, f32[8,16,64]{2,0,1:T(8,128)S(1)}, f32[8,8,64]{2,0,1:T(8,128)S(1)}, s32[8,7]{1,0:T(8,128)S(1)}, f32[8,7,64,64]{3,2,1,0:T(8,128)}, /...) while((s32[]{:T(128)}, f32[8,16,64]{2,0,1:T(8,128)S(1)}, ...), condition=%wide.region_13.15_spmd, body=%wide.region_12.14_spmd.sunk | while | flops 3150896 | bytes 322845 | solution.py:71
  183.1 16.7 %while.487 = (s32[]{:T(128)}, f32[8,16,64]{2,0,1:T(8,128)S(1)}, f32[8,8,64]{2,0,1:T(8,128)S(1)}, s32[8,7]{1,0:T(8,128)S(1)}, f32[8,7,64,64]{3,2,1,0:T(8,128)}, /...) while((s32[]{:T(128)}, f32[8,16,64]{2,0,1:T(8,128)S(1)}, ...), condition=%wide.region_15.17_spmd, body=%wide.region_14.16_spmd.sunk | while | flops 3150896 | bytes 322845 | solution.py:71
  337.6 30.9 %all_gather.24 = f32[64,512]{1,0:T(8,128)S(1)} all-gather(f32[8,512]{1,0:T(8,128)S(1)} %reshape.66), channel_id=1, replica_groups=mesh['rows'=64,'rhs'=8] {'rhs'}, dimensions={0}, use_global_device_ids=true | all-gather | bytes 147456 | tf_op jit(solution)/shard_map/all_gather | solution.py:112
  373.2 24.6 %all_gather.26 = f32[64,512]{1,0:T(8,128)S(1)} all-gather(f32[8,512]{1,0:T(8,128)S(1)} %reshape.67), channel_id=1, replica_groups=mesh['rows'=64,'rhs'=8] {'rhs'}, dimensions={0}, use_global_device_ids=true | all-gather | bytes 147456 | tf_op jit(solution)/shard_map/all_gather | solution.py:122
  397.8 126.1 %all-reduce.29 = (f32[64,8]{0,1:T(8,128)S(1)}, f32[64,8]{0,1:T(8,128)S(1)}) all-reduce(f32[64,8]{0,1:T(8,128)S(1)} %fusion.476, f32[64,8]{0,1:T(8,128)S(1)} %fusion.475), channel_id=1, replica_groups=mesh['rows'=64,'rhs'=8] {'rows'}, use_global_device_ids=true, to_apply=%region_35.39 | all-reduce | flops 1024 | bytes 8192 | tf_op jit(solution)/shard_map/psum | solution.py:115
  523.9 24.5 %all_gather.25 = f32[64,64]{0,1:T(8,128)S(1)} all-gather(f32[64,8]{0,1:T(8,128)S(1)} %get-tuple-element.5610), channel_id=1, replica_groups=mesh['rows'=64,'rhs'=8] {'rhs'}, dimensions={1}, use_global_device_ids=true | all-gather | bytes 18432 | tf_op jit(solution)/shard_map/all_gather | solution.py:116
  561.3 16.7 %while.496 = (s32[]{:T(128)}, f32[8,16,64]{2,0,1:T(8,128)S(1)}, f32[8,8,64]{2,0,1:T(8,128)S(1)}, s32[8,7]{1,0:T(8,128)S(1)}, f32[8,7,64,64]{3,2,1,0:T(8,128)}, /...) while((s32[]{:T(128)}, f32[8,16,64]{2,0,1:T(8,128)S(1)}, ...), condition=%wide.region_37.43_spmd, body=%wide.region_36.42_spmd.sunk | while | flops 3150896 | bytes 322845 | solution.py:71
  586.6 16.7 %while.497 = (s32[]{:T(128)}, f32[8,16,64]{2,0,1:T(8,128)S(1)}, f32[8,8,64]{2,0,1:T(8,128)S(1)}, s32[8,7]{1,0:T(8,128)S(1)}, f32[8,7,64,64]{3,2,1,0:T(8,128)}, /...) while((s32[]{:T(128)}, f32[8,16,64]{2,0,1:T(8,128)S(1)}, ...), condition=%wide.region_39.45_spmd, body=%wide.region_38.44_spmd.sunk | while | flops 3150896 | bytes 322845 | solution.py:71
  611.9 16.7 %while.498 = (s32[]{:T(128)}, f32[8,16,64]{2,0,1:T(8,128)S(1)}, f32[8,8,64]{2,0,1:T(8,128)S(1)}, s32[8,7]{1,0:T(8,128)S(1)}, f32[8,7,64,64]{3,2,1,0:T(8,128)}, /...) while((s32[]{:T(128)}, f32[8,16,64]{2,0,1:T(8,128)S(1)}, ...), condition=%wide.region_41.47_spmd, body=%wide.region_40.46_spmd.sunk | while | flops 3150896 | bytes 322845 | solution.py:71
  662.5 16.7 %while.500 = (s32[]{:T(128)}, f32[8,16,64]{2,0,1:T(8,128)S(1)}, f32[8,8,64]{2,0,1:T(8,128)S(1)}, s32[8,7]{1,0:T(8,128)S(1)}, f32[8,7,64,64]{3,2,1,0:T(8,128)}, /...) while((s32[]{:T(128)}, f32[8,16,64]{2,0,1:T(8,128)S(1)}, ...), condition=%wide.region_45.51_spmd, body=%wide.region_44.50_spmd.sunk | while | flops 3150896 | bytes 322845 | solution.py:71
  687.8 16.7 %while.501 = (s32[]{:T(128)}, f32[8,16,64]{2,0,1:T(8,128)S(1)}, f32[8,8,64]{2,0,1:T(8,128)S(1)}, s32[8,7]{1,0:T(8,128)S(1)}, f32[8,7,64,64]{3,2,1,0:T(8,128)}, /...) while((s32[]{:T(128)}, f32[8,16,64]{2,0,1:T(8,128)S(1)}, ...), condition=%wide.region_47.53_spmd, body=%wide.region_46.52_spmd.sunk | while | flops 3150896 | bytes 322845 | solution.py:71
  713.1 16.7 %while.502 = (s32[]{:T(128)}, f32[8,16,64]{2,0,1:T(8,128)S(1)}, f32[8,8,64]{2,0,1:T(8,128)S(1)}, s32[8,7]{1,0:T(8,128)S(1)}, f32[8,7,64,64]{3,2,1,0:T(8,128)}, /...) while((s32[]{:T(128)}, f32[8,16,64]{2,0,1:T(8,128)S(1)}, ...), condition=%wide.region_49.55_spmd, body=%wide.region_48.54_spmd.sunk | while | flops 3150896 | bytes 322845 | solution.py:71
  738.4 16.7 %while.503 = (s32[]{:T(128)}, f32[8,16,64]{2,0,1:T(8,128)S(1)}, f32[8,8,64]{2,0,1:T(8,128)S(1)}, s32[8,7]{1,0:T(8,128)S(1)}, f32[8,7,64,64]{3,2,1,0:T(8,128)}, /...) while((s32[]{:T(128)}, f32[8,16,64]{2,0,1:T(8,128)S(1)}, ...), condition=%wide.region_51.57_spmd, body=%wide.region_50.56_spmd.sunk | while | flops 3150896 | bytes 322845 | solution.py:71
  884.2 37.4 %all-gather.1 = f32[64,64,8]{1,2,0:T(8,128)S(1)} all-gather(f32[1,64,8]{1,2,0:T(8,128)S(1)} %convolution_bitcast_fusion.50), channel_id=2, replica_groups=mesh['rows'=64,'rhs'=8] {'rows'}, dimensions={0}, use_global_device_ids=true | all-gather | bytes 133120 | tf_op jit(solution)/shard_map/all_gather | solution.py:126
  931.0 24.6 %all_gather.29 = f32[64,512]{1,0:T(8,128)S(1)} all-gather(f32[8,512]{1,0:T(8,128)S(1)} %convolution_add_fusion.1), channel_id=1, replica_groups=mesh['rows'=64,'rhs'=8] {'rhs'}, dimensions={0}, use_global_device_ids=true | all-gather | bytes 147456 | tf_op jit(solution)/shard_map/all_gather | solution.py:112
  958.7 24.6 %all_gather.31 = f32[64,512]{1,0:T(8,128)S(1)} all-gather(f32[8,512]{1,0:T(8,128)S(1)} %reshape.71), channel_id=1, replica_groups=mesh['rows'=64,'rhs'=8] {'rhs'}, dimensions={0}, use_global_device_ids=true | all-gather | bytes 147456 | tf_op jit(solution)/shard_map/all_gather | solution.py:133
  983.3 126.1 %all-reduce.28 = (f32[64,8]{0,1:T(8,128)S(1)}, f32[64,8]{0,1:T(8,128)S(1)}) all-reduce(f32[64,8]{0,1:T(8,128)S(1)} %fusion.479, f32[64,8]{0,1:T(8,128)S(1)} %fusion.478), channel_id=1, replica_groups=mesh['rows'=64,'rhs'=8] {'rows'}, use_global_device_ids=true, to_apply=%region_70.76 | all-reduce | flops 1024 | bytes 8192 | tf_op jit(solution)/shard_map/psum | solution.py:115
  1109.4 24.5 %all_gather.30 = f32[64,64]{0,1:T(8,128)S(1)} all-gather(f32[64,8]{0,1:T(8,128)S(1)} %get-tuple-element.5608), channel_id=1, replica_groups=mesh['rows'=64,'rhs'=8] {'rhs'}, dimensions={1}, use_global_device_ids=true | all-gather | bytes 18432 | tf_op jit(solution)/shard_map/all_gather | solution.py:116
  (1524 shorter events, 860.4 us)
Async XLA Ops:
  22.7 8.6 collective-permute-start
  48.0 8.6 collective-permute-start.1
  73.3 8.6 collective-permute-start.2
  98.6 8.6 collective-permute-start.3
  123.9 8.6 collective-permute-start.4
  149.2 8.6 collective-permute-start.5
  174.5 8.6 collective-permute-start.6
  221.8 8.6 collective-permute-start.8
  257.4 8.6 collective-permute-start.10
  293.0 8.6 collective-permute-start.12
  328.7 40.0 %collective-permute-start.14 = (f32[8,512]{1,0:T(8,128)S(1)}, f32[8,512]{1,0:T(8,128)S(1)}, u32[]{:S(2)}, u32[]{:S(2)}) collective-permute-start(f32[8,512]{1,0:T(8,128)S(1)} %reshape.66), channel_id=1, source_target_pairs={{0,8},{8,16},{16,24},{24,32},{32,40},{40,48},{48,56},{56,64},{64,7... | collective-permute-start | bytes 49160 | tf_op jit(solution)/shard_map/ppermute | solution.py:21
  330.6 38.2 %collective-permute-start.15 = (f32[8,512]{1,0:T(8,128)S(1)}, f32[8,512]{1,0:T(8,128)S(1)}, u32[]{:S(2)}, u32[]{:S(2)}) collective-permute-start(f32[8,512]{1,0:T(8,128)S(1)} %reshape.66), channel_id=1, source_target_pairs={{8,0},{16,8},{24,16},{32,24},{40,32},{48,40},{56,48},{64,56},{72,6... | collective-permute-start | bytes 49160 | tf_op jit(solution)/shard_map/ppermute | solution.py:24
  578.0 8.6 collective-permute-start.16
  603.3 8.6 collective-permute-start.17
  628.6 8.6 collective-permute-start.18
  653.9 8.6 collective-permute-start.19
  679.2 8.6 collective-permute-start.20
  704.5 8.6 collective-permute-start.21
  729.8 8.6 collective-permute-start.22
  777.1 8.6 collective-permute-start.24
  794.9 8.6 collective-permute-start.25
  812.7 8.6 collective-permute-start.26
  922.1 33.6 %collective-permute-start.30 = (f32[8,512]{1,0:T(8,128)S(1)}, f32[8,512]{1,0:T(8,128)S(1)}, u32[]{:S(2)}, u32[]{:S(2)}) collective-permute-start(f32[8,512]{1,0:T(8,128)S(1)} %convolution_add_fusion.1), channel_id=1, source_target_pairs={{0,8},{8,16},{16,24},{24,32},{32,40},{40,48},{48,56},{56,64},{64,7... | collective-permute-start | bytes 49160 | tf_op jit(solution)/shard_map/ppermute | solution.py:21
  924.4 31.4 %collective-permute-start.31 = (f32[8,512]{1,0:T(8,128)S(1)}, f32[8,512]{1,0:T(8,128)S(1)}, u32[]{:S(2)}, u32[]{:S(2)}) collective-permute-start(f32[8,512]{1,0:T(8,128)S(1)} %convolution_add_fusion.1), channel_id=1, source_target_pairs={{8,0},{16,8},{24,16},{32,24},{40,32},{48,40},{56,48},{64,56},{72,6... | collective-permute-start | bytes 49160 | tf_op jit(solution)/shard_map/ppermute | solution.py:24
  (11 other events, 191.9 us)
